TPU v7x, 128 devices: a whole 4x4x4 slice. The times are simulated.
128 devices in a mesh: scen: 4 (over x), path: 32 (over z, y, core).
Axes of the slice: x: 4, y: 4, z: 4, core: 2. Of those that a mesh axis runs over, the one named last changes fastest.
Arguments:
- states: float32 [4, 36, 8, 16384], P('scen', None, None, 'path'), may hold values from -1.5 to 1.5
- exercise_dates: int32 [4, 2], P('scen'), may hold values from 0 to 35, as said below
- itm_mask: int32 [4, 2, 16384], P('scen', None, 'path'), may hold values 0 or 1
- surrender: float32 [4, 36, 16384], P('scen', None, 'path'), may hold values from -0.5 to 1
- terminal: float32 [4, 16384], P('scen', 'path'), may hold values from -5 to 5
- discount: float32 [4, 2], P('scen'), may hold values from 0.5 to 1
- ls_table: int32 [256, 8], replicated, may hold values from 0 to 2, as said below
- proxy_table: int32 [2048, 8], replicated, may hold values from 0 to 2, as said below
Outputs:
- path_values: float32 [4, 16384], P('scen', 'path')
- coefficients: float32 [4, 2, 256], P('scen')
- proxy_gram: float32 [2048, 2048], P(('scen', 'path'))
- proxy_rhs: float32 [2048], P(('scen', 'path'))
Inputs may be any that keep to these rules, and one draw needn't show every extreme that they name: `exercise_dates`: the first exercise date lies below 18 and the second at or above it. `ls_table`: no two rows are equal. `proxy_table`: no two rows are equal.
All inputs are finite; a program needn't handle non-finite values. No bound on the sum of `itm_mask` on one device may be relied on, other than what follows from the above.
Results may differ from a plain program's by a relative error of at most 0.005.
Values sent between devices are 32-bit elements; how exact they have to be, the bound alone decides.
A program may use at most 64 MiB of HBM per device.

v0:
```python
import jax
import jax.numpy as jnp
import numpy as np
from jax import lax
from jax.sharding import PartitionSpec as P


def hermite(current):
    return jnp.stack(
        [jnp.ones_like(current), current, (current * current - 1.0) * 0.7071067811865476], axis=-2
    )


def selectors(table):
    levels_iota = jnp.arange(3, dtype=jnp.int32)
    return [
        (table[:, column][:, None] == levels_iota[None, :]).astype(jnp.float32)
        for column in range(table.shape[1])
    ]


def basis_of(levels, picks, form):
    result = jnp.einsum(form, picks[0], levels[:, 0], precision=lax.Precision.HIGHEST)
    for column in range(1, len(picks)):
        result = result * jnp.einsum(
            form, picks[column], levels[:, column], precision=lax.Precision.HIGHEST
        )
    return result


def at_dates(array, moments):
    shaped = moments.reshape((moments.shape[0],) + (1,) * (array.ndim - 1))
    return jnp.take_along_axis(array, shaped, axis=1)[:, 0]


def on_device(
    states, exercise_dates, itm_mask, surrender, terminal, discount, ls_table, proxy_table
):
    scen_count = states.shape[0]
    paths = states.shape[3]
    terms = ls_table.shape[0]
    total_paths = paths * lax.axis_size("path")
    total_rows = scen_count * paths * lax.axis_size("scen") * lax.axis_size("path")
    ls_picks = selectors(ls_table)
    proxy_picks = selectors(proxy_table)
    upper_rows, upper_cols = np.triu_indices(terms)
    position = np.zeros((terms, terms), np.int64)
    position[upper_rows, upper_cols] = np.arange(upper_rows.shape[0])
    position = np.where(
        np.arange(terms)[:, None] <= np.arange(terms)[None, :], position, position.T
    ).reshape(-1)
    identity = jnp.eye(terms, dtype=jnp.float32)

    def solve_one(system, rhs):
        factor = jnp.linalg.cholesky(system)
        return jax.scipy.linalg.cho_solve((factor, True), rhs)

    values = terminal
    found = [None, None]
    for backward in (1, 0):
        moments = exercise_dates[:, backward]
        current = at_dates(states, moments)
        design = basis_of(hermite(current), ls_picks, "ke,ser->skr").astype(jnp.bfloat16)
        values = discount[:, backward][:, None] * values
        live = itm_mask[:, backward, :]
        weighted = design * live.astype(jnp.bfloat16)[:, None, :]
        gram_part = jnp.einsum("skr,slr->skl", weighted, design, preferred_element_type=jnp.float32)
        rhs_part = jnp.sum(weighted.astype(jnp.float32) * values[:, None, :], axis=2)
        gram, rhs = lax.psum((gram_part, rhs_part), "path")
        system = gram / total_paths + 0.05 * identity[None]
        coef = jax.vmap(solve_one)(system, rhs / total_paths)
        found[backward] = coef
        continuation = jnp.einsum(
            "sk,skr->sr", coef, design.astype(jnp.float32), precision=lax.Precision.HIGHEST
        )
        payoff = at_dates(surrender, moments)
        values = jnp.where(live > 0, jnp.maximum(payoff, continuation), values)
    coefficients = jnp.stack(found, axis=1)
    early_states = at_dates(states, exercise_dates[:, 0])
    proxy_design = basis_of(hermite(early_states), proxy_picks, "ke,ser->ksr").astype(jnp.bfloat16)
    proxy_design = proxy_design.reshape(proxy_design.shape[0], scen_count * paths)
    scale = 1.0 / total_rows
    product = lax.dot_general(
        proxy_design, proxy_design, (((1,), (1,)), ((), ())), preferred_element_type=jnp.float32
    )
    proxy_gram = lax.psum_scatter(
        product * scale, ("scen", "path"), scatter_dimension=0, tiled=True
    )
    flat_values = values.reshape(scen_count * paths).astype(jnp.bfloat16)
    rhs_term = jnp.dot(proxy_design, flat_values, preferred_element_type=jnp.float32) * scale
    proxy_rhs = lax.psum_scatter(rhs_term, ("scen", "path"), scatter_dimension=0, tiled=True)
    return (values, coefficients, proxy_gram, proxy_rhs)


def solution(mesh):
    placed = (
        P("scen", None, None, "path"),
        P("scen", None),
        P("scen", None, "path"),
        P("scen", None, "path"),
        P("scen", "path"),
        P("scen", None),
        P(),
        P(),
    )
    return jax.shard_map(
        on_device,
        mesh=mesh,
        in_specs=placed,
        out_specs=(
            P("scen", "path"),
            P("scen", None, None),
            P(("scen", "path"), None),
            P(("scen", "path")),
        ),
        check_vma=False,
    )
```

profile of v0, /device:TPU:1, one launch (start us, length us, event | category | flops | bytes accessed | tf_op | source)
XLA Modules:
  0.0 742.7 jit_solution(15212986259249649768)
XLA Ops:
  8.0 1.3 fusion.132
  13.2 1.0 fusion.130
  14.3 0.8 convert_reduce_fusion
  15.0 1.3 fusion.131
  16.3 0.7 add_multiply_fusion
  18.2 1.2 broadcast_multiply_fusion.1
  22.8 1.1 convolution_bitcast_fusion
  27.2 1.1 convolution_bitcast_fusion.1
  28.3 0.6 reduce-scatter.2.cloned.1.call-start
  28.9 1.9 fusion.18
  30.8 1.9 fusion.17
  32.7 1.9 fusion.16
  34.7 1.9 fusion.15
  36.6 1.9 fusion.14
  38.5 3.5 fusion.12
  42.0 3.4 fusion.13
  45.4 7.1 multiply_convert_fusion
  52.5 12.5 %convolution_multiply_fusion = f32[2048,2048]{1,0:T(8,128)} fusion(bf16[2048,512]{1,0:T(8,128)(2,1)} %multiply_convert_fusion), kind=kOutput, calls=%fused_computation.4 | convolution fusion | flops 4299161600 | bytes 18874368 | tf_op jit(solution)/shard_map/dot_general | solution.py:83
  69.0 65.8 %psum.30 = f32[1,256]{1,0:T(1,128)S(1)} all-reduce(f32[1,256]{1,0:T(1,128)S(1)} %bitcast.415), channel_id=1, replica_groups=mesh['scen'=4,'path'=32] {'path'}, use_global_device_ids=true, to_apply=%region_7.11 | all-reduce | flops 256 | bytes 2048 | tf_op jit(solution)/shard_map/psum | solution.py:69
  134.8 0.7 broadcast_select_fusion
  135.5 0.6 multiply_bitcast_fusion.1
  136.1 1.0 all-reduce.5.cloned.1.call-done
  137.1 1.0 select_add_fusion.1
  138.2 1.0 fusion.35
  139.2 11.7 %custom-call.19 = f32[1,128,128]{2,1,0:T(8,128)S(1)} custom-call(f32[1,128,128]{2,1,0:T(8,128)S(1)} %cholesky.191), custom_call_target="Cholesky" | custom-call | tf_op jit(solution)/shard_map/vmap(jit(cholesky))/cholesky | solution.py:55
  151.0 0.5 select_reduce_fusion.3
  151.5 9.8 %custom-call.20 = f32[1,1,128,128]{2,3,1,0:T(8,128)S(1)} custom-call(f32[1,1,128,128]{3,2,1,0:T(8,128)S(1)} %get-tuple-element.93), custom_call_target="InvertDiagBlocksLowerTriangular" | custom-call | tf_op jit(solution)/shard_map/vmap(jit(cholesky))/cholesky | solution.py:55
  161.8 12.3 %custom-call.21 = f32[1,128,128]{2,1,0:T(8,128)} custom-call(f32[1,128,128]{2,1,0:T(8,128)S(1)} %fusion.2), custom_call_target="Cholesky" | custom-call | tf_op jit(solution)/shard_map/vmap(jit(cholesky))/cholesky | solution.py:55
  174.2 1.0 select_add_fusion
  175.3 1.0 fusion.33
  176.3 0.7 copy-done.1
  177.0 11.9 %custom-call.22 = f32[1,128,128]{2,1,0:T(8,128)S(1)} custom-call(f32[1,128,128]{2,1,0:T(8,128)S(1)} %cholesky.194), custom_call_target="Cholesky" | custom-call | tf_op jit(solution)/shard_map/vmap(jit(cholesky))/cholesky | solution.py:55
  189.0 9.8 %custom-call.23 = f32[1,1,128,128]{2,3,1,0:T(8,128)S(1)} custom-call(f32[1,1,128,128]{3,2,1,0:T(8,128)S(1)} %get-tuple-element.89), custom_call_target="InvertDiagBlocksLowerTriangular" | custom-call | tf_op jit(solution)/shard_map/vmap(jit(cholesky))/cholesky | solution.py:55
  198.8 1.0 bitcast_dynamic-update-slice_fusion.2
  199.9 1.1 fusion.3
  201.0 11.7 %custom-call.24 = f32[1,128,128]{2,1,0:T(8,128)S(1)} custom-call(f32[1,128,128]{2,1,0:T(8,128)S(1)} %fusion.3), custom_call_target="Cholesky" | custom-call | tf_op jit(solution)/shard_map/vmap(jit(cholesky))/cholesky | solution.py:55
  212.7 0.6 compare_reduce_fusion.1
  213.4 0.7 compare_reduce_fusion
  215.4 3.9 while.6
  215.4 0.6 fusion.148
  216.0 1.3 bitcast_dynamic-update-slice_fusion.6
  217.4 0.6 fusion.148
  218.0 1.3 bitcast_dynamic-update-slice_fusion.6
  219.4 19.7 %custom-call.25 = f32[1,2,128,128]{2,3,1,0:T(8,128)S(1)} custom-call(f32[1,2,128,128]{3,2,1,0:T(8,128)S(1)} %bitcast.377), custom_call_target="InvertDiagBlocksLowerTriangular" | custom-call | tf_op jit(solution)/shard_map/vmap(jit(_cho_solve))/triangular_solve | solution.py:56
  239.1 1.3 compare_reduce_fusion.3
  240.4 0.9 select_reduce_fusion.2
  241.3 0.6 compare_reduce_fusion.2
  243.2 5.3 while.7
  243.2 0.7 constant_dynamic-slice_fusion.5
  243.9 0.6 fusion.149
  244.5 1.3 bitcast_dynamic-update-slice_fusion.7
  245.9 0.7 constant_dynamic-slice_fusion.5
  246.6 0.6 fusion.149
  247.1 1.3 bitcast_dynamic-update-slice_fusion.7
  248.5 20.0 %custom-call.26 = f32[1,2,128,128]{2,3,1,0:T(8,128)S(1)} custom-call(f32[1,2,128,128]{3,2,1,0:T(8,128)S(1)} %bitcast.376), custom_call_target="InvertDiagBlocksLowerTriangular" | custom-call | tf_op jit(solution)/shard_map/vmap(jit(_cho_solve))/triangular_solve | solution.py:56
  268.5 0.8 fusion.62
  269.3 0.8 fusion.11
  271.3 1.9 fusion.113
  273.4 66.2 %psum.31 = f32[1,256]{1,0:T(1,128)S(1)} all-reduce(f32[1,256]{1,0:T(1,128)S(1)} %bitcast.416), channel_id=1, replica_groups=mesh['scen'=4,'path'=32] {'path'}, use_global_device_ids=true, to_apply=%region_9.14 | all-reduce | flops 256 | bytes 2048 | tf_op jit(solution)/shard_map/psum | solution.py:69
  341.1 0.6 fusion.114
  341.7 65.3 %all-reduce.1 = f32[2048]{0:T(1024)S(1)} all-reduce(f32[2048]{0:T(1024)S(1)} %broadcast_multiply_fusion), channel_id=3, replica_groups=mesh['scen'=4,'path'=32] {'scen','path'}, use_global_device_ids=true, to_apply=%region_11.16.clone | all-reduce | flops 2048 | bytes 16384
  407.0 0.6 dynamic-slice.20
  407.6 0.6 pad_maximum_fusion.2
  408.2 326.6 %reduce-scatter.2.cloned.1.call-done = f32[16,2048]{1,0:T(8,128)} async-done(((f32[2048,2048]{1,0:T(8,128)}), f32[16,2048]{1,0:T(8,128)}) %reduce-scatter.2.cloned.1.call-update) | async-done | bytes 131088 | tf_op jit(solution)/shard_map/reduce_scatter | solution.py:86
  (72 shorter events, 11.7 us)
Async XLA Ops:
  8.0 129.1 %all-reduce.5.cloned.1.call-start = ((), (), s32[]{:S(2)}) async-start(), calls=%async_computation.2 | async-start | bytes 1048576 | tf_op jit(solution)/shard_map/psum | solution.py:69
  23.9 5.0 copy-start.2
  28.3 706.5 %reduce-scatter.2.cloned.1.call-start = ((), (), s32[]{:S(2)}) async-start(), calls=%async_computation.1 | async-start | bytes 16908288 | tf_op jit(solution)/shard_map/reduce_scatter | solution.py:86
  139.2 132.1 %copy-start.3 = (s32[1,2,512]{2,1,0:T(2,128)S(1)}, s32[1,2,512]{2,1,0:T(2,128)}, u32[]{:S(2)}) copy-start(s32[1,2,512]{2,1,0:T(2,128)} %param.17) | copy-start | bytes 12292
  161.3 179.7 %copy-start = (bf16[2048,512]{1,0:T(8,128)(2,1)S(1)}, bf16[2048,512]{1,0:T(8,128)(2,1)}, u32[]{:S(2)}) copy-start(bf16[2048,512]{1,0:T(8,128)(2,1)} %multiply_convert_fusion) | copy-start | bytes 6291460
  176.3 0.7 copy-start.1
  219.4 23.8 %copy-start.5 = (s32[2,2]{1,0:T(2,128)}, s32[2,2]{1,0:T(2,128)S(1)}, u32[]{:S(2)}) copy-start(s32[2,2]{1,0:T(2,128)S(1)} %get-tuple-element.242) | copy-start | bytes 52
  341.1 393.7 %copy-start.4 = (f32[1,512]{1,0:T(1,128)}, f32[1,512]{1,0:T(1,128)S(1)}, u32[]{:S(2)}) copy-start(f32[1,512]{1,0:T(1,128)S(1)} %bitcast_select_fusion.1) | copy-start | bytes 6148
Sparse Core Ops, SparseCore 0:
  28.4 108.6 all-reduce.4
Sparse Core Ops, SparseCore 1:
  65.2 669.6 reduce-scatter.1
where the time goes:
time: 756 us; the launch traced here: 743 us
  waiting for transfers between devices  328 us (43%)
  blocking collectives  197 us (26%)
  other arithmetic  123 us (16%)
  matrix products  53.3 us (7%)
  between operations  26.7 us (4%)
  local copies, waits for them, and re-layouts  14.5 us (2%)
    reduce_scatter x1, waiting for transfers between devices, on_device(): lax.psum_scatter(product * scale, ('scen', 'path'), scatter_dimension=0,...  327 us
    psum x2, blocking collectives, on_device(): gram, rhs = lax.psum((gram_part, rhs_part), 'path')  132 us
    another operation x14, other arithmetic, solve_one(): factor = jnp.linalg.cholesky(system)  72.1 us
    unnamed x1, blocking collectives  65.3 us
    another operation x5, other arithmetic, solve_one(): return jax.scipy.linalg.cho_solve((factor, True), rhs)  39.7 us
    dot_general x21, matrix products, basis_of(): jnp.einsum(form, picks[column], levels[:, column], precision=lax.Precisio...  26.6 us
  transfers between devices with their start and end apart: 2, of which 2 were waited for; matrix products, arithmetic and copies ran while one was open for 23% of the time, Pallas kernels for 0%

commit v1 on v0

v1 whole, which is shorter than its diff:
```python
import functools

import jax
import jax.numpy as jnp
from jax import lax
from jax.experimental import pallas as pl
from jax.experimental.pallas import tpu as pltpu
from jax.sharding import PartitionSpec as P

MESH = pl.DeviceIdType.MESH
HI = lax.Precision.HIGHEST
F32, BF16 = jnp.float32, jnp.bfloat16
ROOT_HALF = 0.7071067811865476
SIDE = 640
OWN = 5
PAIRS = 96
STEP = 32


def nt(a, b):
    return lax.dot_general(a, b, (((1,), (1,)), ((), ())), preferred_element_type=F32)


def nn(a, b):
    return jnp.dot(a, b, preferred_element_type=F32)


def halves(x):
    high = x.astype(BF16)
    return high, (x - high.astype(F32)).astype(BF16)


def three_rows(x):
    high = x.astype(BF16).astype(F32)
    rest = x - high
    mid = rest.astype(BF16).astype(F32)
    sub = lax.broadcasted_iota(jnp.int32, (8, x.shape[1]), 0)
    low = rest - mid
    return jnp.where(
        sub == 0, high, jnp.where(sub == 1, mid, jnp.where(sub == 2, low, 0.0))
    ).astype(BF16)


def add_rows(x):
    return x[0:1] + x[1:2] + x[2:3]


def products(factors, pair_a, pair_b, out, levels):
    count = levels * levels
    for i in range(levels):
        for j in range(levels):
            row = i * levels + j
            pair_a[row : row + 1, :] = factors[0][i] * factors[1][j]
            pair_b[row : row + 1, :] = factors[2][i] * factors[3][j]
    for i in range(count):
        out[i * count : (i + 1) * count, :] = pair_a[i : i + 1, :] * pair_b[0:count, :]


def local_kernel(
    dates, disc, early, late, mask, terminal, table, design_out, gram_out, rhs_out, moment_out,
    pair_a, pair_b, left, right, whole,
):
    paths = terminal.shape[1]
    for backward, block in ((0, early), (1, late)):
        u = block[0, 0]
        h = (u * u - 1.0) * ROOT_HALF
        for top in range(0, table.shape[0], 32):
            t = table[top : top + 32, :]
            result = None
            for v in range(8):
                degree = jnp.broadcast_to(t[:, v : v + 1], (32, paths))
                level = jnp.where(
                    degree == 1, u[v : v + 1, :], jnp.where(degree == 2, h[v : v + 1, :], 1.0)
                )
                result = level if result is None else result * level
            design_out[backward, top : top + 32, :] = result.astype(BF16)
        design = design_out[backward]
        weighted = design * mask[backward : backward + 1, :].astype(F32).astype(BF16)
        gram = nt(weighted, design)
        gram_out[backward, 0:128, :] = gram[0:128, 0:128]
        gram_out[backward, 128:256, :] = gram[128:256, 0:128]
        gram_out[backward, 256:384, :] = gram[128:256, 128:256]
        if backward == 1:
            values = disc[1] * terminal[...]
            rhs_out[...] = add_rows(nt(three_rows(values), weighted))
    u = early[0, 0]
    g = u * u - 1.0
    one = jnp.ones((1, paths), F32)
    def levels(v):
        x, y = u[v : v + 1, :], g[v : v + 1, :]
        return [one, x, y, x * y, y * y]
    for side, first in ((left, 0), (right, 4)):
        side[624:SIDE, :] = jnp.zeros((SIDE - 624, paths), F32)
        products([levels(first + v) for v in range(4)], pair_a, pair_b, side, 5)
    lh, ll = halves(left[...])
    rh, rl = halves(right[...])
    whole[...] = nt(lh, rh) + nt(lh, rl) + nt(ll, rh)
    for b in range(SIDE // OWN):
        moment_out[b] = whole[b * OWN : (b + 1) * OWN, :]


def exchange_kernel(
    paths, scens, ls, rhs, mom, ls_out, rhs_out, mom_out,
    ls_in, rhs_in, mom_half, mom_acc, mom_in,
    ls_s, ls_r, rhs_s, rhs_r, ag_s, ag_r, half_s, half_r, mom_s, mom_r,
):
    s, p = lax.axis_index("scen"), lax.axis_index("path")
    core, seat = p % 2, p // 2
    seats = paths // 2
    group = scens * seats
    me = s * seats + seat

    def path_peer(d):
        return (p + d) % paths

    def core_peer(d):
        return (me + d) % group

    def core_id(j):
        return (j // seats, (j % seats) * 2 + core)

    barrier = pltpu.get_barrier_semaphore()

    @pl.loop(1, paths)
    def _(d):
        pl.semaphore_signal(barrier, inc=1, device_id=(s, path_peer(d)), device_id_type=MESH)

    @pl.loop(1, group)
    def _(d):
        pl.semaphore_signal(barrier, inc=1, device_id=core_id(core_peer(d)), device_id_type=MESH)

    pl.semaphore_wait(barrier, paths - 1 + group - 1)

    def half_copy():
        return pltpu.make_async_remote_copy(
            src_ref=mom.at[1 - core], dst_ref=mom_half, send_sem=half_s, recv_sem=half_r,
            device_id=(s, seat * 2 + 1 - core), device_id_type=MESH)

    def ls_copy(q):
        return pltpu.make_async_remote_copy(
            src_ref=ls.at[q], dst_ref=ls_in.at[p], send_sem=ls_s.at[q], recv_sem=ls_r.at[p],
            device_id=(s, q), device_id_type=MESH)

    def rhs_copy(q):
        return pltpu.make_async_remote_copy(
            src_ref=rhs, dst_ref=rhs_in.at[p], send_sem=rhs_s.at[q], recv_sem=rhs_r.at[p],
            device_id=(s, q), device_id_type=MESH)

    def ag_copy(q):
        return pltpu.make_async_remote_copy(
            src_ref=ls_out.at[p], dst_ref=ls_out.at[p], send_sem=ag_s.at[q], recv_sem=ag_r.at[p],
            device_id=(s, q), device_id_type=MESH)

    def mom_copy(j):
        return pltpu.make_async_remote_copy(
            src_ref=mom_acc.at[j], dst_ref=mom_in.at[me], send_sem=mom_s.at[j], recv_sem=mom_r.at[me],
            device_id=core_id(j), device_id_type=MESH)

    def arrived(buffer, sems, slot):
        pltpu.make_async_copy(buffer.at[slot], buffer.at[slot], sems.at[slot]).wait()

    half_copy().start()

    @pl.loop(1, paths)
    def _(d):
        ls_copy(path_peer(d)).start()
        rhs_copy(path_peer(d)).start()

    @pl.loop(1, paths)
    def _(d):
        arrived(ls_in, ls_r, path_peer(d))
        arrived(rhs_in, rhs_r, path_peer(d))

    def add_ls(d, carry):
        return carry[0] + ls_in[path_peer(d)], carry[1] + rhs_in[path_peer(d)]

    total, rhs_total = lax.fori_loop(1, paths, add_ls, (ls[p], rhs[...]))
    ls_out[p] = total
    rhs_out[...] = rhs_total

    @pl.loop(1, paths)
    def _(d):
        ag_copy(path_peer(d)).start()

    half_copy().wait()

    @pl.loop(0, group)
    def _(j):
        mom_acc[j] = mom[core, j] + mom_half[j]

    @pl.loop(1, group)
    def _(d):
        mom_copy(core_peer(d)).start()

    @pl.loop(1, paths)
    def _(d):
        arrived(ls_out, ag_r, path_peer(d))

    @pl.loop(1, group)
    def _(d):
        arrived(mom_in, mom_r, core_peer(d))

    def add_mom(d, carry):
        return carry + mom_in[core_peer(d)]

    mom_out[...] = lax.fori_loop(1, group, add_mom, mom_acc[me])

    @pl.loop(1, paths)
    def _(d):
        ls_copy(path_peer(d)).wait_send()
        rhs_copy(path_peer(d)).wait_send()
        ag_copy(path_peer(d)).wait_send()

    @pl.loop(1, group)
    def _(d):
        mom_copy(core_peer(d)).wait_send()


def second_kernel(
    paths, scens, rhs, mom, rhs_out, full, rhs_in,
    own_s, rhs_s, rhs_r, mom_s, mom_r, half_s, half_r,
):
    s, p = lax.axis_index("scen"), lax.axis_index("path")
    core, seat = p % 2, p // 2
    seats = paths // 2
    group = scens * seats
    me = s * seats + seat

    def path_peer(d):
        return (p + d) % paths

    def core_peer(d):
        return (me + d) % group

    def core_id(j):
        return (j // seats, (j % seats) * 2 + core)

    barrier = pltpu.get_barrier_semaphore()

    @pl.loop(1, paths)
    def _(d):
        pl.semaphore_signal(barrier, inc=1, device_id=(s, path_peer(d)), device_id_type=MESH)

    @pl.loop(1, group)
    def _(d):
        pl.semaphore_signal(barrier, inc=1, device_id=core_id(core_peer(d)), device_id_type=MESH)

    pl.semaphore_wait(barrier, paths - 1 + group - 1)

    def rhs_copy(q):
        return pltpu.make_async_remote_copy(
            src_ref=rhs, dst_ref=rhs_in.at[p], send_sem=rhs_s.at[q], recv_sem=rhs_r.at[p],
            device_id=(s, q), device_id_type=MESH)

    def mom_copy(j):
        return pltpu.make_async_remote_copy(
            src_ref=mom, dst_ref=full.at[core, me], send_sem=mom_s.at[j], recv_sem=mom_r.at[me],
            device_id=core_id(j), device_id_type=MESH)

    def half_copy():
        return pltpu.make_async_remote_copy(
            src_ref=full.at[core], dst_ref=full.at[core], send_sem=half_s, recv_sem=half_r,
            device_id=(s, seat * 2 + 1 - core), device_id_type=MESH)

    @pl.loop(1, paths)
    def _(d):
        rhs_copy(path_peer(d)).start()

    @pl.loop(1, group)
    def _(d):
        mom_copy(core_peer(d)).start()

    own = pltpu.make_async_copy(mom, full.at[core, me], own_s)
    own.start()

    @pl.loop(1, paths)
    def _(d):
        slot = path_peer(d)
        pltpu.make_async_copy(rhs_in.at[slot], rhs_in.at[slot], rhs_r.at[slot]).wait()

    def add_rhs(d, carry):
        return carry + rhs_in[path_peer(d)]

    rhs_out[...] = lax.fori_loop(1, paths, add_rhs, rhs[...])
    own.wait()

    @pl.loop(1, group)
    def _(d):
        slot = core_peer(d)
        pltpu.make_async_copy(full.at[core, slot], full.at[core, slot], mom_r.at[slot]).wait()

    half_copy().start()
    half_copy().wait()

    @pl.loop(1, paths)
    def _(d):
        rhs_copy(path_peer(d)).wait_send()

    @pl.loop(1, group)
    def _(d):
        mom_copy(core_peer(d)).wait_send()


def third_kernel(paths, scens, parts, out, parts_in, mine, mine_in, a_s, a_r, b_s, b_r):
    s, p = lax.axis_index("scen"), lax.axis_index("path")

    def path_peer(d):
        return (p + d) % paths

    def scen_peer(d):
        return (s + d) % scens

    barrier = pltpu.get_barrier_semaphore()

    @pl.loop(1, paths)
    def _(d):
        pl.semaphore_signal(barrier, inc=1, device_id=(s, path_peer(d)), device_id_type=MESH)

    @pl.loop(1, scens)
    def _(d):
        pl.semaphore_signal(barrier, inc=1, device_id=(scen_peer(d), p), device_id_type=MESH)

    pl.semaphore_wait(barrier, paths - 1 + scens - 1)

    def a_copy(q):
        return pltpu.make_async_remote_copy(
            src_ref=parts.at[q], dst_ref=parts_in.at[p], send_sem=a_s.at[q], recv_sem=a_r.at[p],
            device_id=(s, q), device_id_type=MESH)

    def b_copy(t):
        return pltpu.make_async_remote_copy(
            src_ref=mine.at[t], dst_ref=mine_in.at[s], send_sem=b_s.at[t], recv_sem=b_r.at[s],
            device_id=(t, p), device_id_type=MESH)

    @pl.loop(1, paths)
    def _(d):
        a_copy(path_peer(d)).start()

    @pl.loop(1, paths)
    def _(d):
        slot = path_peer(d)
        pltpu.make_async_copy(parts_in.at[slot], parts_in.at[slot], a_r.at[slot]).wait()

    def add_a(d, carry):
        return carry + parts_in[path_peer(d)]

    mine[...] = lax.fori_loop(1, paths, add_a, parts[p])

    @pl.loop(1, scens)
    def _(d):
        b_copy(scen_peer(d)).start()

    @pl.loop(1, scens)
    def _(d):
        slot = scen_peer(d)
        pltpu.make_async_copy(mine_in.at[slot], mine_in.at[slot], b_r.at[slot]).wait()

    def add_b(d, carry):
        return carry + mine_in[scen_peer(d)]

    out[...] = lax.fori_loop(1, scens, add_b, mine[s])

    @pl.loop(1, paths)
    def _(d):
        a_copy(path_peer(d)).wait_send()

    @pl.loop(1, scens)
    def _(d):
        b_copy(scen_peer(d)).wait_send()


def sweep_small(e, n):
    def at(i, j):
        return e[min(i, j), max(i, j)]

    for k in range(0, n, 2):
        p, q, s = e[k, k], e[k, k + 1], e[k + 1, k + 1]
        w = 1.0 / (p * s - q * q)
        pw, qw, sw = p * w, q * w, s * w
        others = [i for i in range(n) if i not in (k, k + 1)]
        r0 = {i: at(k, i) for i in others}
        r1 = {i: at(k + 1, i) for i in others}
        x0 = {i: sw * r0[i] - qw * r1[i] for i in others}
        x1 = {i: pw * r1[i] - qw * r0[i] for i in others}
        for i in others:
            for j in others:
                if i <= j:
                    e[i, j] = e[i, j] - (r0[i] * x0[j] + r1[i] * x1[j])
        for i in others:
            e[min(i, k), max(i, k)] = x0[i]
            e[min(i, k + 1), max(i, k + 1)] = x1[i]
        e[k, k], e[k, k + 1], e[k + 1, k + 1] = -sw, qw, -pw
    return e


def tree_sum(terms):
    while len(terms) > 1:
        terms = [terms[t] + terms[t + 1] for t in range(0, len(terms), 2)]
    return terms[0]


def leaf(a, e_ref, r_ref):
    lane = lax.broadcasted_iota(jnp.int32, (STEP, 128), 1)
    lane8 = lax.broadcasted_iota(jnp.int32, (8, 128), 1)
    sub8 = lax.broadcasted_iota(jnp.int32, (8, 128), 0)
    half = lane - lane % 64
    in_half = lane8 % 64
    for o in range(0, STEP, 8):
        cols = [jnp.take_along_axis(a, half + (o + j), axis=1) for j in range(8)]
        r_ref[...] = a[o : o + 8, :]
        for j in range(8):
            e_ref[j] = cols[j][o : o + 8, :]
        e = {(i, j): e_ref[j, pl.ds(i, 8, stride=0), :] for i in range(8) for j in range(i, 8)}
        e = sweep_small(e, 8)
        rows = [r_ref[pl.ds(i, 8, stride=0), :] for i in range(8)]
        xs = []
        for i in range(8):
            entries = [e[min(i, j), max(i, j)] for j in range(8)]
            x = -tree_sum([entries[j] * rows[j] for j in range(8)])
            for j in range(8):
                x = jnp.where(in_half == o + j, entries[j], x)
            xs.append(x)
        tile = xs[0]
        for i in range(1, 8):
            tile = jnp.where(sub8 == i, xs[i], tile)
        inside = (in_half >= o) & (in_half < o + 8)
        tiles = []
        for t in range(0, STEP, 8):
            if t == o:
                tiles.append(tile)
            else:
                base = jnp.where(inside, 0.0, a[t : t + 8, :])
                tiles.append(base - tree_sum([cols[j][t : t + 8, :] * xs[j] for j in range(8)]))
        a = jnp.concatenate(tiles, axis=0)
    return a


def invert(a_ref, e_ref, r_ref):
    n = a_ref.shape[1]
    lane = lax.broadcasted_iota(jnp.int32, (STEP, n), 1)
    lane1 = lax.broadcasted_iota(jnp.int32, (STEP, 128), 1)
    lane2 = lax.broadcasted_iota(jnp.int32, (n - STEP, n), 1)

    def body(k, _):
        first = [a_ref[d, 0:STEP, 0:128] for d in range(2)]
        both = leaf(jnp.where(lane1 < 64, first[0], pltpu.roll(first[1], 64, 1)), e_ref, r_ref)
        for d, neg in enumerate((both, pltpu.roll(both, 64, 1))):
            r = a_ref[d, 0:STEP, :]
            rest = a_ref[d, STEP:, :]
            x = jnp.dot(neg[:, 0:STEP], r, precision=HI, preferred_element_type=F32)
            xt = jnp.where(lane < STEP, jnp.concatenate([neg, neg], axis=1), -x)
            new = jnp.where(lane2 < STEP, 0.0, rest) - jnp.dot(
                rest[:, 0:STEP], xt, precision=HI, preferred_element_type=F32
            )
            a_ref[d, 0 : n - STEP, :] = pltpu.roll(new, n - STEP, 1)
            a_ref[d, n - STEP :, :] = pltpu.roll(xt, n - STEP, 1)
        return 0

    lax.fori_loop(0, n // STEP, body, 0)


def solve_kernel(
    total, dates, disc, gram, rhs, design, mask, surrender, terminal,
    coef_out, inv_out, values_out, rhs_out, a_ref, e_ref, r_ref,
):
    n = a_ref.shape[1]
    scale = 1.0 / total
    ri = lax.broadcasted_iota(jnp.int32, (128, 128), 0)
    ci = lax.broadcasted_iota(jnp.int32, (128, 128), 1)
    ridge = jnp.where(ri == ci, 0.05, 0.0)
    for d in range(2):
        corner = gram[d, 128:256, :] * scale
        a_ref[d, 0:128, 0:128] = gram[d, 0:128, :] * scale + ridge
        a_ref[d, 128:256, 0:128] = corner
        a_ref[d, 0:128, 128:256] = corner.T
        a_ref[d, 128:256, 128:256] = gram[d, 256:384, :] * scale + ridge
    invert(a_ref, e_ref, r_ref)
    inv_out[...] = -a_ref[0]
    side = jnp.broadcast_to(rhs[...] * scale, (8, n))
    coef = -jnp.dot(side, a_ref[1], precision=HI, preferred_element_type=F32)
    coef_out[...] = coef[0:1]
    continuation = add_rows(nn(three_rows(coef[0:1]), design[1]))
    payoff = surrender[pl.ds(dates[1], 1), :]
    values = disc[1] * terminal[...]
    values = jnp.where(mask[1:2, :] > 0, jnp.maximum(payoff, continuation), values)
    values = disc[0] * values
    values_out[...] = values
    weighted = design[0] * mask[0:1, :].astype(F32).astype(BF16)
    rhs_out[...] = add_rows(nt(three_rows(values), weighted))


def one_hots(table_t, low_out, high_out):
    row = lax.broadcasted_iota(jnp.int32, low_out.shape, 0)
    for first, out in ((0, low_out), (4, high_out)):
        t = [table_t[first + v : first + v + 1, :] for v in range(4)]
        code = ((t[0] * 3 + t[1]) * 3 + t[2]) * 3 + t[3]
        out[...] = jnp.where(row == code, 1.0, 0.0).astype(out.dtype)


def tail_kernel(
    total, dates, inv, rhs, design, mask, surrender, values, early, table_t,
    values_out, coef_out, rhs_out, pair_a, pair_b, left, right, low, high,
):
    n = inv.shape[0]
    paths = values.shape[1]
    side = jnp.broadcast_to(rhs[...] * (1.0 / total), (8, n))
    coef = jnp.dot(side, inv[...], precision=HI, preferred_element_type=F32)[0:1]
    coef_out[...] = coef
    continuation = add_rows(nn(three_rows(coef), design[0]))
    payoff = surrender[pl.ds(dates[0], 1), :]
    final = jnp.where(mask[0:1, :] > 0, jnp.maximum(payoff, continuation), values[...])
    values_out[...] = final
    u = early[0, 0]
    h = (u * u - 1.0) * ROOT_HALF
    one = jnp.ones((1, paths), F32)
    for out, first in ((left, 0), (right, 4)):
        out[80:PAIRS, :] = jnp.zeros((PAIRS - 80, paths), F32)
        levels = [[one, u[first + v : first + v + 1, :], h[first + v : first + v + 1, :]] for v in range(4)]
        products(levels, pair_a, pair_b, out, 3)
    rounded = final.astype(BF16).astype(F32)
    lh, ll = halves(left[...] * rounded)
    rh, rl = halves(right[...])
    one_hots(table_t, low, high)
    wh, wl = halves(nt(rh, lh) + nt(rh, ll) + nt(rl, lh))
    picked = (nn(wh, low[...]) + nn(wl, low[...])) * high[...]
    rhs_out[...] = jnp.sum(picked, axis=0, keepdims=True)


def gram_kernel(total, mine, full, table_t, out, whole, both, pattern, pick_l, pick_r, low, high):
    row = lax.broadcasted_iota(jnp.int32, (PAIRS, 1), 0)
    lane = lax.broadcasted_iota(jnp.int32, (1, SIDE), 1)
    for v, (three, five) in enumerate(((27, 125), (9, 25), (3, 5), (1, 1))):
        b = jnp.where(row < 81, (row // three) % 3, -9)
        m = jnp.where(lane < 625, (lane // five) % 5, -20)
        b, m = jnp.broadcast_to(b, (PAIRS, SIDE)), jnp.broadcast_to(m, (PAIRS, SIDE))
        ones = ((b == 0) & (m == 1)) | ((b == 1) & ((m == 0) | (m == 2))) | ((b == 2) & (m == 3))
        pattern[v, 0] = jnp.where(m == b, 1.0, 0.0).astype(BF16)
        pattern[v, 1] = jnp.where(ones, 1.0, 0.0).astype(BF16)
        pattern[v, 2] = jnp.where(m == b + 2, 1.0, 0.0).astype(BF16)
    for b in range(SIDE // OWN):
        whole[b * OWN : (b + 1) * OWN, :] = full[b]
    mh, ml = halves(whole[...])
    both[0] = mh
    both[1] = ml
    one_hots(table_t, low, high)
    scale = None
    for v in range(8):
        factor = jnp.where(table_t[v : v + 1, :] == 2, ROOT_HALF, 1.0)
        scale = factor if scale is None else scale * factor

    @pl.loop(0, out.shape[0])
    def _(r):
        def pattern_of(first):
            result = None
            for v in range(4):
                block = pattern[v, mine[r * 8 + first + v]]
                result = block if result is None else result * block
            return result

        own = 1.0 / total
        for v in range(8):
            own = own * jnp.where(mine[r * 8 + v] == 2, ROOT_HALF, 1.0)
        pick_l[...] = pattern_of(0)
        pick_r[...] = pattern_of(4)
        yh, yl = halves(nn(pick_l[...], both[0]) + nn(pick_l[...], both[1]))
        zh, zl = halves(nt(pick_r[...], yh) + nt(pick_r[...], yl))
        picked = (nn(zh, low[...]) + nn(zl, low[...])) * high[...]
        out[pl.ds(r, 1), :] = jnp.sum(picked, axis=0, keepdims=True) * scale * own


VMEM = pl.BlockSpec(memory_space=pltpu.VMEM)
SMEM = pl.BlockSpec(memory_space=pltpu.SMEM)
DMA = pltpu.SemaphoreType.DMA


def on_device(
    states, exercise_dates, itm_mask, surrender, terminal, discount, ls_table, proxy_table
):
    scens, path_devices = lax.axis_size("scen"), lax.axis_size("path")
    paths = states.shape[3]
    terms, proxy_terms = ls_table.shape[0], proxy_table.shape[0]
    devices = scens * path_devices
    total_paths = paths * path_devices
    total_rows = total_paths * scens
    dates, disc = exercise_dates[0], discount[0]
    mask, payoffs = itm_mask[0], surrender[0]
    table_t = proxy_table.T
    own_rows = proxy_terms // devices
    index = lax.axis_index("scen") * path_devices + lax.axis_index("path")
    mine = lax.dynamic_slice(proxy_table, (index * own_rows, 0), (own_rows, 8)).reshape(-1)

    def state_spec(j):
        return pl.BlockSpec((1, 1, 8, paths), lambda i, d: (0, d[j], 0, 0))

    early_spec = state_spec(0)
    design, gram, rhs, moments = pl.pallas_call(
        local_kernel,
        grid_spec=pltpu.PrefetchScalarGridSpec(
            num_scalar_prefetch=1,
            grid=(1,),
            in_specs=[SMEM, early_spec, state_spec(1), VMEM, VMEM, VMEM],
            out_specs=[VMEM] * 4,
            scratch_shapes=[
                pltpu.VMEM((32, paths), F32),
                pltpu.VMEM((32, paths), F32),
                pltpu.VMEM((SIDE, paths), F32),
                pltpu.VMEM((SIDE, paths), F32),
                pltpu.VMEM((SIDE, SIDE), F32),
            ],
        ),
        out_shape=(
            jax.ShapeDtypeStruct((2, terms, paths), BF16),
            jax.ShapeDtypeStruct((2, 384, 128), F32),
            jax.ShapeDtypeStruct((1, terms), F32),
            jax.ShapeDtypeStruct((devices, OWN, SIDE), F32),
        ),
        name="local",
    )(dates, disc, states, states, mask, terminal, ls_table)

    half = devices // 2
    rows = 768 // path_devices
    gram, rhs, block = pl.pallas_call(
        functools.partial(exchange_kernel, path_devices, scens),
        out_shape=(
            jax.ShapeDtypeStruct((path_devices, rows, 128), F32),
            jax.ShapeDtypeStruct((1, terms), F32),
            jax.ShapeDtypeStruct((OWN, SIDE), F32),
        ),
        in_specs=[VMEM] * 3,
        out_specs=[VMEM] * 3,
        scratch_shapes=[
            pltpu.VMEM((path_devices, rows, 128), F32),
            pltpu.VMEM((path_devices, 1, terms), F32),
            pltpu.VMEM((half, OWN, SIDE), F32),
            pltpu.VMEM((half, OWN, SIDE), F32),
            pltpu.VMEM((half, OWN, SIDE), F32),
            DMA((path_devices,)), DMA((path_devices,)),
            DMA((path_devices,)), DMA((path_devices,)),
            DMA((path_devices,)), DMA((path_devices,)),
            DMA, DMA,
            DMA((half,)), DMA((half,)),
        ],
        compiler_params=pltpu.CompilerParams(collective_id=0, has_side_effects=True),
        name="exchange",
    )(gram.reshape(path_devices, rows, 128), rhs, moments.reshape(2, half, OWN, SIDE))

    coef_late, inv, values, rhs = pl.pallas_call(
        functools.partial(solve_kernel, total_paths),
        out_shape=(
            jax.ShapeDtypeStruct((1, terms), F32),
            jax.ShapeDtypeStruct((terms, terms), F32),
            jax.ShapeDtypeStruct((1, paths), F32),
            jax.ShapeDtypeStruct((1, terms), F32),
        ),
        in_specs=[SMEM, SMEM] + [VMEM] * 6,
        out_specs=[VMEM] * 4,
        scratch_shapes=[
            pltpu.VMEM((2, terms, terms), F32),
            pltpu.VMEM((8, 8, 128), F32),
            pltpu.VMEM((8, 128), F32),
        ],
        name="solve",
    )(dates, disc, gram.reshape(2, 384, 128), rhs, design, mask, payoffs, terminal)

    rhs, full = pl.pallas_call(
        functools.partial(second_kernel, path_devices, scens),
        out_shape=(
            jax.ShapeDtypeStruct((1, terms), F32),
            jax.ShapeDtypeStruct((2, half, OWN, SIDE), F32),
        ),
        in_specs=[VMEM] * 2,
        out_specs=[VMEM] * 2,
        scratch_shapes=[
            pltpu.VMEM((path_devices, 1, terms), F32),
            DMA,
            DMA((path_devices,)), DMA((path_devices,)),
            DMA((half,)), DMA((half,)),
            DMA, DMA,
        ],
        compiler_params=pltpu.CompilerParams(collective_id=1, has_side_effects=True),
        name="second",
    )(rhs, block)

    values, coef_early, proxy_part = pl.pallas_call(
        functools.partial(tail_kernel, total_paths),
        grid_spec=pltpu.PrefetchScalarGridSpec(
            num_scalar_prefetch=1,
            grid=(1,),
            in_specs=[VMEM] * 6 + [early_spec, VMEM],
            out_specs=[VMEM] * 3,
            scratch_shapes=[
                pltpu.VMEM((16, paths), F32),
                pltpu.VMEM((16, paths), F32),
                pltpu.VMEM((PAIRS, paths), F32),
                pltpu.VMEM((PAIRS, paths), F32),
                pltpu.VMEM((PAIRS, proxy_terms), BF16),
                pltpu.VMEM((PAIRS, proxy_terms), F32),
            ],
        ),
        out_shape=(
            jax.ShapeDtypeStruct((1, paths), F32),
            jax.ShapeDtypeStruct((1, terms), F32),
            jax.ShapeDtypeStruct((1, proxy_terms), F32),
        ),
        name="tail",
    )(dates, inv, rhs, design, mask, payoffs, values, states, table_t)

    parts = proxy_part.reshape(scens, path_devices, 1, own_rows).transpose(1, 0, 2, 3)
    parts = jnp.pad(parts, ((0, 0), (0, 0), (0, 0), (0, 128 - own_rows)))
    proxy_rhs = pl.pallas_call(
        functools.partial(third_kernel, path_devices, scens),
        out_shape=jax.ShapeDtypeStruct((1, 128), F32),
        in_specs=[VMEM],
        out_specs=VMEM,
        scratch_shapes=[
            pltpu.VMEM((path_devices, scens, 1, 128), F32),
            pltpu.VMEM((scens, 1, 128), F32),
            pltpu.VMEM((scens, 1, 128), F32),
            DMA((path_devices,)), DMA((path_devices,)),
            DMA((scens,)), DMA((scens,)),
        ],
        compiler_params=pltpu.CompilerParams(collective_id=2, has_side_effects=True),
        name="third",
    )(parts)

    proxy_gram = pl.pallas_call(
        functools.partial(gram_kernel, total_rows),
        grid_spec=pltpu.PrefetchScalarGridSpec(
            num_scalar_prefetch=1,
            grid=(1,),
            in_specs=[VMEM] * 2,
            out_specs=VMEM,
            scratch_shapes=[
                pltpu.VMEM((SIDE, SIDE), F32),
                pltpu.VMEM((2, SIDE, SIDE), BF16),
                pltpu.VMEM((4, 3, PAIRS, SIDE), BF16),
                pltpu.VMEM((PAIRS, SIDE), BF16),
                pltpu.VMEM((PAIRS, SIDE), BF16),
                pltpu.VMEM((PAIRS, proxy_terms), BF16),
                pltpu.VMEM((PAIRS, proxy_terms), F32),
            ],
        ),
        out_shape=jax.ShapeDtypeStruct((own_rows, proxy_terms), F32),
        name="gram",
    )(mine, full.reshape(devices, OWN, SIDE), table_t)

    coefficients = jnp.stack([coef_early, coef_late], axis=1)
    return (values, coefficients, proxy_gram, proxy_rhs[0, :own_rows] * (1.0 / total_rows))


def solution(mesh):
    placed = (
        P("scen", None, None, "path"),
        P("scen", None),
        P("scen", None, "path"),
        P("scen", None, "path"),
        P("scen", "path"),
        P("scen", None),
        P(),
        P(),
    )
    return jax.shard_map(
        on_device,
        mesh=mesh,
        in_specs=placed,
        out_specs=(
            P("scen", "path"),
            P("scen", None, None),
            P(("scen", "path"), None),
            P(("scen", "path")),
        ),
        check_vma=False,
    )
```

time: 756 us -> 156 us (0.21); the launches traced: 743 us -> 155 us
  waiting for transfers between devices: 328 us -> 0 us
  blocking collectives: 197 us -> 0 us
  Pallas kernels: 0 us -> 147 us
  other arithmetic: 123 us -> 3.13 us
  matrix products: 53.3 us -> 0 us
  between operations: 26.7 us -> 0.7 us
  local copies, waits for them, and re-layouts: 14.5 us -> 4.94 us
    reduce_scatter x1 -> x0, waiting for transfers between devices: 327 us -> none  [on_device(): lax.psum_scatter(product * scale, ('scen', 'path'), scatter_dimension=0,...]
    pallas_call x0 -> x7, Pallas kernels: none -> 147 us  [the longest x1 48.5 us: on_device(): pl.pallas_call(functools.partial(exchange_kernel, path_devices, scens), o...]
    psum x2 -> x0, blocking collectives: 132 us -> none  [on_device(): gram, rhs = lax.psum((gram_part, rhs_part), 'path')]
    another operation x23 -> x1, other arithmetic: 112 us -> 0.59 us  [on_device(): coefficients = jnp.stack([coef_early, coef_late], axis=1)]
    unnamed x1 -> x0, blocking collectives: 65.3 us -> none
    dot_general x30 -> x0, matrix products: 47.1 us -> none  [the longest x21 26.6 us: basis_of(): jnp.einsum(form, picks[column], levels[:, column], precision=lax.Precisio...]
    another operation x20 -> x0, local copies, waits for them, and re-layouts: 9.26 us -> none  [the longest x15 9.21 us: solve_one(): return jax.scipy.linalg.cho_solve((factor, True), rhs)]
  transfers between devices with their start and end apart: 2 -> 0, of which waited for: 2 -> 0; matrix products, arithmetic and copies ran while one was open for 23% -> 0% of each run, Pallas kernels for 0% -> 0%
where the time goes in v1:
time: 156 us; the launch traced here: 155 us
  Pallas kernels  147 us (94%)
  local copies, waits for them, and re-layouts  4.94 us (3%)
  other arithmetic  3.13 us (2%)
    pallas_call x1, Pallas kernels, on_device(): pl.pallas_call(functools.partial(exchange_kernel, path_devices, scens), o...  48.5 us
    pallas_call x1, Pallas kernels, on_device(): pl.pallas_call(functools.partial(second_kernel, path_devices, scens), out...  35.8 us
    pallas_call x1, Pallas kernels, on_device(): pl.pallas_call(functools.partial(gram_kernel, total_rows), grid_spec=pltp...  21.6 us
    pallas_call x1, Pallas kernels, on_device(): pl.pallas_call(functools.partial(solve_kernel, total_paths), out_shape=(j...  16.3 us
    pallas_call x1, Pallas kernels, on_device(): pl.pallas_call(functools.partial(third_kernel, path_devices, scens), out_...  14.3 us
    pallas_call x1, Pallas kernels, on_device(): pl.pallas_call(local_kernel, grid_spec=pltpu.PrefetchScalarGridSpec(num_s...  6.57 us
    pallas_call x1, Pallas kernels, on_device(): pl.pallas_call(functools.partial(tail_kernel, total_paths), grid_spec=plt...  3.6 us

profile of v1, /device:TPU:1, one launch (start us, length us, event | category | flops | bytes accessed | tf_op | source)
XLA Modules:
  0.0 155.4 jit_solution(13384965257388648298)
XLA Ops:
  0.6 0.0 copy-start
  0.6 1.5 copy.14.table
  2.2 6.6 %local.1 = (bf16[2,256,512]{2,1,0:T(8,128)(2,1)}, f32[2,384,128]{2,1,0:T(8,128)}, f32[1,256]{1,0:T(1,128)}, f32[128,5,640]{2,1,0:T(8,128)}) custom-call(s32[2]{0:T(128)} %bitcast.30, f32[2]{0:T(128)} %bitcast.33, f32[1,36,8,512]{3,2,1,0:T(8,128)} %early.3, f32[1,36,8,512]{3,2,1,0:T(8,128)} %early.3, s32[2,512]{1,0:T(2,128)} %bitcast.27, f32[1,512]{1,0:T(1,128)} %terminal.3, ...), custom_call_target="tpu_custom_call" | custom-call | tf_op jit(solution)/shard_map/local/pallas_call | solution.py:596
  8.7 48.5 %exchange.1 = (f32[32,24,128]{2,1,0:T(8,128)}, f32[1,256]{1,0:T(1,128)}, f32[5,640]{1,0:T(8,128)}) custom-call(f32[32,24,128]{2,1,0:T(8,128)} %bitcast.23, f32[1,256]{1,0:T(1,128)} %get-tuple-element.21.rhs, f32[2,64,5,640]{3,2,1,0:T(8,128)} %bitcast.19), custom_call_target="tpu_custom_call" | custom-call | tf_op jit(solution)/shard_map/exchange/pallas_call | solution.py:622
  57.2 0.0 copy-done
  57.2 0.6 copy.20
  57.8 16.3 %solve.1 = (f32[1,256]{1,0:T(1,128)}, f32[256,256]{1,0:T(8,128)}, f32[1,512]{1,0:T(1,128)}, f32[1,256]{1,0:T(1,128)}) custom-call(s32[2]{0:T(128)} %bitcast.31, f32[2]{0:T(128)} %bitcast.34, f32[2,384,128]{2,1,0:T(8,128)} %bitcast.22, f32[1,256]{1,0:T(1,128)} %get-tuple-element.24.rhs, bf16[2,256,512]{2,1,0:T(8,128)(2,1)} %get-tuple-element.25.design, ...), custom_call_target="tpu_custom_call" | custom-call | tf_op jit(solution)/shard_map/solve/pallas_call | solution.py:647
  74.2 0.0 copy-start.1
  74.2 35.8 %second.1 = (f32[1,256]{1,0:T(1,128)}, f32[2,64,5,640]{3,2,1,0:T(8,128)}) custom-call(f32[1,256]{1,0:T(1,128)} %get-tuple-element.27.rhs, f32[5,640]{1,0:T(8,128)} %get-tuple-element.28.mom), custom_call_target="tpu_custom_call" | custom-call | tf_op jit(solution)/shard_map/second/pallas_call | solution.py:665
  110.0 3.6 %tail.1 = (f32[1,512]{1,0:T(1,128)}, f32[1,256]{1,0:T(1,128)}, f32[1,2048]{1,0:T(1,128)}) custom-call(s32[2]{0:T(128)} %bitcast.32, f32[256,256]{1,0:T(8,128)} %get-tuple-element.26.inv, f32[1,256]{1,0:T(1,128)} %get-tuple-element.29.rhs, bf16[2,256,512]{2,1,0:T(8,128)(2,1)} %get-tuple-element.25.design, s32[2,512]{1,0:T(2,128)} %bitcast.29, ...), custom_call_target="tpu_custom_call" | custom-call | tf_op jit(solution)/shard_map/tail/pallas_call | solution.py:684
  113.6 0.0 copy-start.2
  113.6 0.5 broadcast.12
  114.1 1.4 reduce.3
  115.5 0.1 reshape.33
  115.6 0.1 copy.21
  115.6 0.7 pad.4.parts
  116.3 14.3 %third.1 = f32[1,128]{1,0:T(1,128)} custom-call(f32[32,4,1,128]{3,2,1,0:T(1,128)} %pad.4.parts), custom_call_target="tpu_custom_call" | custom-call | tf_op jit(solution)/shard_map/third/pallas_call | solution.py:710
  130.6 1.2 multiply_bitcast_fusion
  131.8 0.8 constant_dynamic-slice_fusion
  132.5 0.1 copy.15
  132.6 0.6 reshape.31.mine
  133.2 21.6 %gram.1 = f32[16,2048]{1,0:T(8,128)} custom-call(s32[128]{0:T(128)} %reshape.31.mine, f32[128,5,640]{2,1,0:T(8,128)} %bitcast.18, s32[8,2048]{1,0:T(8,128)} %bitcast.25), custom_call_target="tpu_custom_call" | custom-call | tf_op jit(solution)/shard_map/gram/pallas_call | solution.py:726
  154.8 0.0 copy-done.1
  154.8 0.0 copy-done.2
  154.8 0.6 pad_maximum_fusion
Async XLA Ops:
  0.6 56.6 %copy-start = (f32[1,36,512]{2,0,1:T(1,128)S(1)}, f32[1,36,512]{2,0,1:T(1,128)}, u32[]{:S(2)}) copy-start(f32[1,36,512]{2,0,1:T(1,128)} %param.11) | copy-start | bytes 221188
  74.2 80.6 %copy-start.1 = (f32[1,256]{1,0:T(1,128)S(1)}, f32[1,256]{1,0:T(1,128)}, u32[]{:S(2)}) copy-start(f32[1,256]{1,0:T(1,128)} %get-tuple-element.33) | copy-start | bytes 3076
  113.6 41.2 %copy-start.2 = (f32[1,256]{1,0:T(1,128)S(1)}, f32[1,256]{1,0:T(1,128)}, u32[]{:S(2)}) copy-start(f32[1,256]{1,0:T(1,128)} %get-tuple-element.32) | copy-start | bytes 3076
